TPU v7x, 512 devices: a whole 4x8x8 slice. The times are simulated.
512 devices in a mesh: cache: 64 (over x, z, core), rank: 8 (over y).
Axes of the slice: x: 4, y: 8, z: 8, core: 2. Of those that a mesh axis runs over, the one named last changes fastest.
Arguments:
- cand_rows: bfloat16 [64, 64, 4, 1024], P('cache', None, None, 'rank'), may hold values from -48 to 48
- listed: int32 [64], replicated, may hold values from 0 to 63, each once
- hist_len: int32 [64], P('cache'), may hold values from 768 to 3072, as said below
- block_mask: int32 [64, 24], P('cache'), may hold values 0 or 1
- hist_keys: bfloat16 [1, 64, 3072, 1024], P(None, 'cache', None, 'rank'), may hold values from -6 to 6
- hist_values: bfloat16 [1, 64, 3072, 1024], P(None, 'cache', None, 'rank'), may hold values from -6 to 6
- w_query: bfloat16 [1, 1024, 1024], P(None, None, 'rank'), may hold values from -0.1875 to 0.1875
- w_gate: bfloat16 [1, 1024, 1024], P(None, None, 'rank'), may hold values from -0.1875 to 0.1875
- w_out: bfloat16 [1, 1024, 1024], P(None, None, 'rank'), may hold values from -0.1875 to 0.1875
Outputs:
- ranked: bfloat16 [64, 64, 4, 1024], P('cache', None, None, 'rank')
Inputs may be any that keep to these rules, and one draw needn't show every extreme that they name: `hist_len`: some user has exactly 3072 history events. `listed`: each user id appears once.
All inputs are finite; a program needn't handle non-finite values. No bound on the sum of `block_mask` on one device may be relied on, other than what follows from the above.
Results may differ from a plain program's by a relative error of at most 0.0024.
Values may be sent and summed in bfloat16 or wider, within the bound.
A program may use at most 64 MiB of HBM per device.

v0:
```python
import jax
import jax.numpy as jnp
from jax import lax
from jax.sharding import PartitionSpec as P

D = 1024
HEADS = 8
BLOCK = 128
EPSILON = 1e-05
GROUP_BLOCKS = 4


def head_norm(values):
    centre = jnp.mean(values, axis=-1, keepdims=True)
    spread = jnp.mean(jnp.square(values - centre), axis=-1, keepdims=True)
    return (values - centre) * lax.rsqrt(spread + EPSILON)


def attend(queries, key_cache, value_cache, length, block_list, block_live, turn_count):
    head_size = queries.shape[-1]
    score_scale = head_size ** (-0.5)
    within = jnp.arange(BLOCK, dtype=jnp.int32)
    running = jnp.zeros(queries.shape, jnp.float32)

    def one_turn(turn_no, running):
        chosen = lax.dynamic_slice_in_dim(block_list, turn_no * GROUP_BLOCKS, GROUP_BLOCKS)
        chosen_live = lax.dynamic_slice_in_dim(block_live, turn_no * GROUP_BLOCKS, GROUP_BLOCKS)
        key_rows = jnp.take(key_cache, chosen, axis=0).reshape(
            GROUP_BLOCKS * BLOCK, key_cache.shape[2], head_size
        )
        value_rows = jnp.take(value_cache, chosen, axis=0).reshape(
            GROUP_BLOCKS * BLOCK, key_cache.shape[2], head_size
        )
        places = (chosen[:, None] * BLOCK + within[None, :]).reshape(GROUP_BLOCKS * BLOCK)
        live_mask = ((places < length) & jnp.repeat(chosen_live, BLOCK)).astype(jnp.float32)
        scores = (
            jnp.einsum("nkhe,the->nkht", queries, key_rows, preferred_element_type=jnp.float32)
            * score_scale
        )
        weights = (jax.nn.silu(scores) * live_mask).astype(jnp.bfloat16)
        return running + jnp.einsum(
            "nkht,the->nkhe", weights, value_rows, preferred_element_type=jnp.float32
        )

    return lax.fori_loop(0, turn_count, one_turn, running)


def finish(result):
    return lax.all_to_all(result, "cache", split_axis=0, concat_axis=1, tiled=True)


def on_device(
    cand_rows, listed, hist_len, block_mask, hist_keys, hist_values, w_query, w_gate, w_out
):
    head_size = D // HEADS
    local_width = w_query.shape[2]
    local_heads = local_width // head_size
    blocks_total = block_mask.shape[1]
    padded = -(-blocks_total // GROUP_BLOCKS) * GROUP_BLOCKS
    slot_of_user = jnp.argsort(listed)
    outgoing = jnp.take(cand_rows, slot_of_user, axis=1)
    length = hist_len[0]
    starts = jnp.arange(blocks_total, dtype=jnp.int32) * BLOCK
    usable = (block_mask[0] == 1) & (starts < length)
    filler = jnp.zeros((padded - blocks_total,), jnp.int32)
    block_list = jnp.concatenate([jnp.arange(blocks_total, dtype=jnp.int32), filler])
    block_live = jnp.concatenate([usable, filler > 0])
    turn_count = padded // GROUP_BLOCKS
    current = lax.all_to_all(outgoing, "cache", split_axis=1, concat_axis=0, tiled=True)
    whole_rows = lax.all_gather(current, "rank", axis=3, tiled=True)
    normed = head_norm(whole_rows.astype(jnp.float32)).astype(jnp.bfloat16)
    queries = jax.nn.silu(
        jnp.einsum("nukd,de->nuke", normed, w_query[0], preferred_element_type=jnp.float32)
    ).astype(jnp.bfloat16)
    gate_act = jax.nn.silu(
        jnp.einsum("nukd,de->nuke", normed, w_gate[0], preferred_element_type=jnp.float32)
    )
    split_shape = queries.shape[:3] + (local_heads, head_size)
    queries = queries.reshape(split_shape)
    length, block_list, block_live, turn_count = (length, block_list, block_live, turn_count)
    key_cache = hist_keys[0, 0].reshape(blocks_total, BLOCK, local_heads, head_size)
    value_cache = hist_values[0, 0].reshape(blocks_total, BLOCK, local_heads, head_size)
    attended_list = [
        attend(queries[:, 0], key_cache, value_cache, length, block_list, block_live, turn_count)
    ]
    attended = jnp.stack(attended_list, axis=1)
    hidden = (
        (head_norm(attended) * gate_act.reshape(split_shape))
        .reshape(queries.shape[:3] + (local_width,))
        .astype(jnp.bfloat16)
    )
    rows_in = w_out[0]
    projected = jnp.einsum(
        "nukd,de->nuke",
        lax.all_gather(hidden, "rank", axis=3, tiled=True),
        rows_in,
        preferred_element_type=jnp.float32,
    )
    current = (current.astype(jnp.float32) + projected).astype(jnp.bfloat16)
    returned = finish(current)
    return jnp.take(returned, listed, axis=1)


def solution(mesh):
    placed = (
        P("cache", None, None, "rank"),
        P(),
        P("cache"),
        P("cache", None),
        P(None, "cache", None, "rank"),
        P(None, "cache", None, "rank"),
        P(None, None, "rank"),
        P(None, None, "rank"),
        P(None, None, "rank"),
    )
    return jax.shard_map(
        on_device,
        mesh=mesh,
        in_specs=placed,
        out_specs=P("cache", None, None, "rank"),
        check_vma=False,
    )
```

profile of v0, /device:TPU:1, one launch (start us, length us, event | category | flops | bytes accessed | tf_op | source)
XLA Modules:
  0.0 122.2 jit_solution(12769290152046905703)
XLA Ops:
  0.0 0.7 copy-done.4
  0.7 2.0 %sort.17 = (s32[64]{0:T(128)}, s32[64]{0:T(128)S(1)}) sort(s32[64]{0:T(128)S(1)} %copy-done.4, s32[64]{0:T(128)S(1)} %iota.13), dimensions={0}, to_apply=%region_0.0 | sort | flops 384 | bytes 1024 | tf_op jit(solution)/shard_map/jit(argsort)/sort | solution.py:60
  2.8 1.5 %gather_fusion.2 = bf16[64,4,128]{2,1,0:T(4,128)(2,1)S(1)} fusion(bf16[64,4,128]{2,1,0:T(4,128)(2,1)} %bitcast.138, s32[1024]{0:T(1024)S(1)} %pad_clamp_fusion.2), kind=kCustom, calls=%fused_computation.clone | custom fusion | bytes 131328 | tf_op jit(solution)/shard_map/jit(_take)/gather | solution.py:61
  4.3 0.8 fusion.45
  5.0 14.8 %all-to-all-start = ((bf16[1,64,4,128]{3,2,0,1:T(4,128)(2,1)}), bf16[1,64,4,128]{3,2,0,1:T(4,128)(2,1)S(1)}, u32[]{:S(2)}, u32[]{:S(2)}) async-start(bf16[1,64,4,128]{3,2,0,1:T(4,128)(2,1)} %fusion.45), calls=%async_computation | async-start | bytes 131072 | tf_op jit(solution)/shard_map/all_to_all | solution.py:69
  21.2 8.5 %all-to-all-done = bf16[1,64,4,128]{3,2,0,1:T(4,128)(2,1)S(1)} async-done(((bf16[1,64,4,128]{3,2,0,1:T(4,128)(2,1)}), bf16[1,64,4,128]{3,2,0,1:T(4,128)(2,1)S(1)}, u32[]{:S(2)}, u32[]{:S(2)}) %all-to-all-start) | async-done | bytes 65568 | tf_op jit(solution)/shard_map/all_to_all | solution.py:69
  29.7 15.8 %all-gather = bf16[1,64,4,1024]{3,2,0,1:T(4,128)(2,1)S(1)} all-gather(bf16[1,64,4,128]{3,2,0,1:T(4,128)(2,1)S(1)} %all-to-all-done), channel_id=2, replica_groups=mesh['cache'=64,'rank'=8] {'rank'}, dimensions={3}, use_global_device_ids=true | all-gather | bytes 589824 | tf_op jit(solution)/shard_map/all_gather | solution.py:70
  47.0 29.7 %while.14 = (s32[]{:T(128)}, f32[64,4,1,128]{3,0,1,2:T(8,128)S(1)}, s32[24]{0:T(128)S(1)}, bf16[24,128,1,128]{3,1,0,2:T(8,128)(2,1)}, bf16[24,128,1,128]{3,1,0,2...) while((s32[]{:T(128)}, f32[64,4,1,128]{3,0,1,2:T(8,128)S(1)}, ...), condition=%wide.region_4.7_spmd.clone, body=%wide.region_3.6_spmd.clone.sunk | while | flops 68226080 | bytes 1646929 | solution.py:45
  47.1 1.7 %gather_fusion = bf16[4,128,128]{2,1,0:T(8,128)(2,1)S(1)} fusion(bf16[24,128,128]{2,1,0:T(8,128)(2,1)} %bitcast.136, s32[1024]{0:T(1024)S(1)} %pad_clamp_fusion.4), kind=kCustom, calls=%fused_computation.3.clone.clone.1 | custom fusion | bytes 262160 | tf_op jit(solution)/shard_map/while/body/eval_jaxpr/jit(_take)/gather | solution.py:28
  48.8 1.7 %gather_fusion.1 = bf16[4,128,128]{2,1,0:T(8,128)(2,1)S(1)} fusion(bf16[24,128,128]{2,1,0:T(8,128)(2,1)} %bitcast.134, s32[1024]{0:T(1024)S(1)} %pad_clamp_fusion.4), kind=kCustom, calls=%fused_computation.1.clone.clone.1 | custom fusion | bytes 262160 | tf_op jit(solution)/shard_map/while/body/eval_jaxpr/jit(_take)/gather | solution.py:31
  50.8 0.7 convert_bitcast_fusion.3
  52.0 1.7 %gather_fusion = bf16[4,128,128]{2,1,0:T(8,128)(2,1)S(1)} fusion(bf16[24,128,128]{2,1,0:T(8,128)(2,1)} %bitcast.136, s32[1024]{0:T(1024)S(1)} %pad_clamp_fusion.4), kind=kCustom, calls=%fused_computation.3.clone.clone.1 | custom fusion | bytes 262160 | tf_op jit(solution)/shard_map/while/body/eval_jaxpr/jit(_take)/gather | solution.py:28
  53.7 1.7 %gather_fusion.1 = bf16[4,128,128]{2,1,0:T(8,128)(2,1)S(1)} fusion(bf16[24,128,128]{2,1,0:T(8,128)(2,1)} %bitcast.134, s32[1024]{0:T(1024)S(1)} %pad_clamp_fusion.4), kind=kCustom, calls=%fused_computation.1.clone.clone.1 | custom fusion | bytes 262160 | tf_op jit(solution)/shard_map/while/body/eval_jaxpr/jit(_take)/gather | solution.py:31
  55.7 0.7 convert_bitcast_fusion.3
  57.0 1.7 %gather_fusion = bf16[4,128,128]{2,1,0:T(8,128)(2,1)S(1)} fusion(bf16[24,128,128]{2,1,0:T(8,128)(2,1)} %bitcast.136, s32[1024]{0:T(1024)S(1)} %pad_clamp_fusion.4), kind=kCustom, calls=%fused_computation.3.clone.clone.1 | custom fusion | bytes 262160 | tf_op jit(solution)/shard_map/while/body/eval_jaxpr/jit(_take)/gather | solution.py:28
  58.7 1.7 %gather_fusion.1 = bf16[4,128,128]{2,1,0:T(8,128)(2,1)S(1)} fusion(bf16[24,128,128]{2,1,0:T(8,128)(2,1)} %bitcast.134, s32[1024]{0:T(1024)S(1)} %pad_clamp_fusion.4), kind=kCustom, calls=%fused_computation.1.clone.clone.1 | custom fusion | bytes 262160 | tf_op jit(solution)/shard_map/while/body/eval_jaxpr/jit(_take)/gather | solution.py:31
  60.7 0.7 convert_bitcast_fusion.3
  61.9 1.7 %gather_fusion = bf16[4,128,128]{2,1,0:T(8,128)(2,1)S(1)} fusion(bf16[24,128,128]{2,1,0:T(8,128)(2,1)} %bitcast.136, s32[1024]{0:T(1024)S(1)} %pad_clamp_fusion.4), kind=kCustom, calls=%fused_computation.3.clone.clone.1 | custom fusion | bytes 262160 | tf_op jit(solution)/shard_map/while/body/eval_jaxpr/jit(_take)/gather | solution.py:28
  63.6 1.7 %gather_fusion.1 = bf16[4,128,128]{2,1,0:T(8,128)(2,1)S(1)} fusion(bf16[24,128,128]{2,1,0:T(8,128)(2,1)} %bitcast.134, s32[1024]{0:T(1024)S(1)} %pad_clamp_fusion.4), kind=kCustom, calls=%fused_computation.1.clone.clone.1 | custom fusion | bytes 262160 | tf_op jit(solution)/shard_map/while/body/eval_jaxpr/jit(_take)/gather | solution.py:31
  65.6 0.7 convert_bitcast_fusion.3
  66.9 1.7 %gather_fusion = bf16[4,128,128]{2,1,0:T(8,128)(2,1)S(1)} fusion(bf16[24,128,128]{2,1,0:T(8,128)(2,1)} %bitcast.136, s32[1024]{0:T(1024)S(1)} %pad_clamp_fusion.4), kind=kCustom, calls=%fused_computation.3.clone.clone.1 | custom fusion | bytes 262160 | tf_op jit(solution)/shard_map/while/body/eval_jaxpr/jit(_take)/gather | solution.py:28
  68.6 1.7 %gather_fusion.1 = bf16[4,128,128]{2,1,0:T(8,128)(2,1)S(1)} fusion(bf16[24,128,128]{2,1,0:T(8,128)(2,1)} %bitcast.134, s32[1024]{0:T(1024)S(1)} %pad_clamp_fusion.4), kind=kCustom, calls=%fused_computation.1.clone.clone.1 | custom fusion | bytes 262160 | tf_op jit(solution)/shard_map/while/body/eval_jaxpr/jit(_take)/gather | solution.py:31
  70.6 0.7 convert_bitcast_fusion.3
  71.8 1.7 %gather_fusion = bf16[4,128,128]{2,1,0:T(8,128)(2,1)S(1)} fusion(bf16[24,128,128]{2,1,0:T(8,128)(2,1)} %bitcast.136, s32[1024]{0:T(1024)S(1)} %pad_clamp_fusion.4), kind=kCustom, calls=%fused_computation.3.clone.clone.1 | custom fusion | bytes 262160 | tf_op jit(solution)/shard_map/while/body/eval_jaxpr/jit(_take)/gather | solution.py:28
  73.6 1.7 %gather_fusion.1 = bf16[4,128,128]{2,1,0:T(8,128)(2,1)S(1)} fusion(bf16[24,128,128]{2,1,0:T(8,128)(2,1)} %bitcast.134, s32[1024]{0:T(1024)S(1)} %pad_clamp_fusion.4), kind=kCustom, calls=%fused_computation.1.clone.clone.1 | custom fusion | bytes 262160 | tf_op jit(solution)/shard_map/while/body/eval_jaxpr/jit(_take)/gather | solution.py:31
  75.5 0.7 convert_bitcast_fusion.3
  78.0 19.5 %all-gather.1 = bf16[64,4,1024]{2,0,1:T(8,128)(2,1)S(1)} all-gather(bf16[64,4,128]{2,0,1:T(8,128)(2,1)S(1)} %fusion.31), channel_id=3, replica_groups=mesh['cache'=64,'rank'=8] {'rank'}, dimensions={2}, use_global_device_ids=true | all-gather | bytes 589824 | tf_op jit(solution)/shard_map/all_gather | solution.py:95
  97.8 0.7 copy.46
  98.5 12.4 %all-to-all-start.1 = ((bf16[64,1,4,128]{3,2,1,0:T(4,128)(2,1)}), bf16[64,1,4,128]{3,2,1,0:T(4,128)(2,1)S(1)}, u32[]{:S(2)}, u32[]{:S(2)}) async-start(bf16[64,1,4,128]{3,2,1,0:T(4,128)(2,1)} %copy.46), calls=%async_computation.1 | async-start | bytes 131072 | tf_op jit(solution)/shard_map/all_to_all | solution.py:49
  110.9 9.9 %all-to-all-done.1 = bf16[64,1,4,128]{3,2,1,0:T(4,128)(2,1)S(1)} async-done(((bf16[64,1,4,128]{3,2,1,0:T(4,128)(2,1)}), bf16[64,1,4,128]{3,2,1,0:T(4,128)(2,1)S(1)}, u32[]{:S(2)}, u32[]{:S(2)}) %all-to-all-start.1) | async-done | bytes 65568 | tf_op jit(solution)/shard_map/all_to_all | solution.py:49
  120.8 0.7 gather_fusion.3
  121.4 0.8 bitcast_select_fusion.2
  (67 shorter events, 8.3 us)
Async XLA Ops:
  0.0 46.6 %copy-start = (bf16[1,1024,128]{2,1,0:T(8,128)(2,1)S(1)}, bf16[1,1024,128]{2,1,0:T(8,128)(2,1)}, u32[]{:S(2)}) copy-start(bf16[1,1024,128]{2,1,0:T(8,128)(2,1)} %param.21) | copy-start | bytes 786436
  0.0 0.7 copy-start.4
  5.0 24.6 %all-to-all-start = ((bf16[1,64,4,128]{3,2,0,1:T(4,128)(2,1)}), bf16[1,64,4,128]{3,2,0,1:T(4,128)(2,1)S(1)}, u32[]{:S(2)}, u32[]{:S(2)}) async-start(bf16[1,64,4,128]{3,2,0,1:T(4,128)(2,1)} %fusion.45), calls=%async_computation | async-start | bytes 131072 | tf_op jit(solution)/shard_map/all_to_all | solution.py:69
  20.5 0.7 copy-start.3
  76.7 1.0 copy-start.2
  78.0 19.5 %copy-start.1 = (bf16[1,1024,128]{2,1,0:T(8,128)(2,1)S(1)}, bf16[1,1024,128]{2,1,0:T(8,128)(2,1)}, u32[]{:S(2)}) copy-start(bf16[1,1024,128]{2,1,0:T(8,128)(2,1)} %param.23) | copy-start | bytes 786436
  98.5 22.3 %all-to-all-start.1 = ((bf16[64,1,4,128]{3,2,1,0:T(4,128)(2,1)}), bf16[64,1,4,128]{3,2,1,0:T(4,128)(2,1)S(1)}, u32[]{:S(2)}, u32[]{:S(2)}) async-start(bf16[64,1,4,128]{3,2,1,0:T(4,128)(2,1)} %copy.46), calls=%async_computation.1 | async-start | bytes 131072 | tf_op jit(solution)/shard_map/all_to_all | solution.py:49
where the time goes:
time: 123 us; the launch traced here: 122 us
  blocking collectives  35.3 us (29%)
  starting transfers between devices  27.3 us (22%)
  local copies, waits for them, and re-layouts  25.8 us (21%)
  waiting for transfers between devices  18.3 us (15%)
  other arithmetic  10.9 us (9%)
  matrix products  3.56 us (3%)
    all_gather x1, blocking collectives, on_device(): lax.all_gather(hidden, 'rank', axis=3, tiled=True)  19.5 us
    all_gather x1, blocking collectives, on_device(): whole_rows = lax.all_gather(current, 'rank', axis=3, tiled=True)  15.8 us
    all_to_all x1, starting transfers between devices, on_device(): lax.all_to_all(outgoing, 'cache', split_axis=1, concat_axis=0, tiled=True)  14.8 us
    all_to_all x1, starting transfers between devices, finish(): lax.all_to_all(result, 'cache', split_axis=0, concat_axis=1, tiled=True)  12.4 us
    gather x6, local copies, waits for them, and re-layouts, one_turn(): jnp.take(key_cache, chosen, axis=0)  10.2 us
    gather x6, local copies, waits for them, and re-layouts, one_turn(): jnp.take(value_cache, chosen, axis=0)  10.2 us
    all_to_all x1, waiting for transfers between devices, finish(): lax.all_to_all(result, 'cache', split_axis=0, concat_axis=1, tiled=True)  9.87 us
    all_to_all x1, waiting for transfers between devices, on_device(): lax.all_to_all(outgoing, 'cache', split_axis=1, concat_axis=0, tiled=True)  8.45 us
  transfers between devices with their start and end apart: 2, of which 2 were waited for; matrix products, arithmetic and copies ran while one was open for 0% of the time, Pallas kernels for 0%

commit v1 on v0

--- a/solution.py
+++ b/solution.py
@@ -8,6 +8,22 @@
 BLOCK = 128
 EPSILON = 1e-05
 GROUP_BLOCKS = 4
+
+
+def summed_both_ways(value, axis, dim, term):
+    length, index, rows = (lax.axis_size(axis), lax.axis_index(axis), value.shape[dim])
+    right = [(i, (i + 1) % length) for i in range(length)]
+    left = [(i, (i - 1) % length) for i in range(length)]
+    half = length // 2
+    from_left = from_right = value
+    so_far = term(value, index * rows)
+    for turn in range(1, half + 1):
+        from_left = lax.ppermute(from_left, axis, right)
+        if turn < length - half:
+            from_right = lax.ppermute(from_right, axis, left)
+            so_far = so_far + term(from_right, (index + turn) % length * rows)
+        so_far = so_far + term(from_left, (index - turn) % length * rows)
+    return so_far
 
 
 def head_norm(values):
@@ -90,11 +106,16 @@
         .astype(jnp.bfloat16)
     )
     rows_in = w_out[0]
-    projected = jnp.einsum(
-        "nukd,de->nuke",
-        lax.all_gather(hidden, "rank", axis=3, tiled=True),
-        rows_in,
-        preferred_element_type=jnp.float32,
+    projected = summed_both_ways(
+        hidden,
+        "rank",
+        3,
+        lambda part, start: jnp.einsum(
+            "nukd,de->nuke",
+            part,
+            lax.dynamic_slice_in_dim(rows_in, start, part.shape[3], axis=0),
+            preferred_element_type=jnp.float32,
+        ),
     )
     current = (current.astype(jnp.float32) + projected).astype(jnp.bfloat16)
     returned = finish(current)

time: 123 us -> 130 us (1.057)
  starting transfers between devices: 27.3 us -> 47.3 us
  blocking collectives: 35.3 us -> 15.8 us
  waiting for transfers between devices: 18.3 us -> 22.1 us
    ppermute x0 -> x7, starting transfers between devices: none -> 21.4 us  [the longest x3 13.2 us: summed_both_ways(): from_right = lax.ppermute(from_right, axis, left)]
    all_gather x1 -> x0, blocking collectives: 19.5 us -> none  [on_device(): lax.all_gather(hidden, 'rank', axis=3, tiled=True)]
    ppermute x0 -> x7, waiting for transfers between devices: none -> 3.98 us  [the longest x4 3.97 us: summed_both_ways(): from_left = lax.ppermute(from_left, axis, right)]
    all_to_all x1, starting transfers between devices: 12.4 us -> 11.1 us  [finish(): lax.all_to_all(result, 'cache', split_axis=0, concat_axis=1, tiled=True)]
  transfers between devices with their start and end apart: 2 -> 9, of which waited for: 2 -> 3; matrix products, arithmetic and copies ran while one was open for 0% -> 1% of each run, Pallas kernels for 0% -> 0%
where the time goes in v1:
time: 130 us; the launch traced here: 128 us
  starting transfers between devices  47.3 us (36%)
  local copies, waits for them, and re-layouts  26.3 us (20%)
  waiting for transfers between devices  22.1 us (17%)
  blocking collectives  15.8 us (12%)
  other arithmetic  10.9 us (8%)
  matrix products  4.47 us (3%)
    all_gather x1, blocking collectives, on_device(): whole_rows = lax.all_gather(current, 'rank', axis=3, tiled=True)  15.8 us
    all_to_all x1, starting transfers between devices, on_device(): lax.all_to_all(outgoing, 'cache', split_axis=1, concat_axis=0, tiled=True)  14.8 us
    ppermute x3, starting transfers between devices, summed_both_ways(): from_right = lax.ppermute(from_right, axis, left)  13.2 us
    all_to_all x1, starting transfers between devices, finish(): lax.all_to_all(result, 'cache', split_axis=0, concat_axis=1, tiled=True)  11.1 us
    gather x6, local copies, waits for them, and re-layouts, one_turn(): jnp.take(key_cache, chosen, axis=0)  10.2 us
    gather x6, local copies, waits for them, and re-layouts, one_turn(): jnp.take(value_cache, chosen, axis=0)  10.2 us
    all_to_all x1, waiting for transfers between devices, finish(): lax.all_to_all(result, 'cache', split_axis=0, concat_axis=1, tiled=True)  9.87 us
    all_to_all x1, waiting for transfers between devices, on_device(): lax.all_to_all(outgoing, 'cache', split_axis=1, concat_axis=0, tiled=True)  8.3 us
  transfers between devices with their start and end apart: 9, of which 3 were waited for; matrix products, arithmetic and copies ran while one was open for 1% of the time, Pallas kernels for 0%

profile of v1, /device:TPU:1, one launch (start us, length us, event | category | flops | bytes accessed | tf_op | source)
XLA Modules:
  0.0 128.5 jit_solution(4080672387346761620)
XLA Ops:
  0.7 2.0 %sort.17 = (s32[64]{0:T(128)}, s32[64]{0:T(128)S(1)}) sort(s32[64]{0:T(128)S(1)} %copy-done.4, s32[64]{0:T(128)S(1)} %iota.13), dimensions={0}, to_apply=%region_0.0 | sort | flops 384 | bytes 1024 | tf_op jit(solution)/shard_map/jit(argsort)/sort | solution.py:76
  2.8 1.5 %gather_fusion.2 = bf16[64,4,128]{2,1,0:T(4,128)(2,1)S(1)} fusion(bf16[64,4,128]{2,1,0:T(4,128)(2,1)} %bitcast.190, s32[1024]{0:T(1024)S(1)} %pad_clamp_fusion.2), kind=kCustom, calls=%fused_computation.clone | custom fusion | bytes 131328 | tf_op jit(solution)/shard_map/jit(_take)/gather | solution.py:77
  4.3 0.8 fusion.56
  5.0 14.8 %all-to-all-start = ((bf16[1,64,4,128]{3,2,0,1:T(4,128)(2,1)}), bf16[1,64,4,128]{3,2,0,1:T(4,128)(2,1)S(1)}, u32[]{:S(2)}, u32[]{:S(2)}) async-start(bf16[1,64,4,128]{3,2,0,1:T(4,128)(2,1)} %fusion.56), calls=%async_computation | async-start | bytes 131072 | tf_op jit(solution)/shard_map/all_to_all | solution.py:85
  21.4 8.3 %all-to-all-done = bf16[1,64,4,128]{3,2,0,1:T(4,128)(2,1)S(1)} async-done(((bf16[1,64,4,128]{3,2,0,1:T(4,128)(2,1)}), bf16[1,64,4,128]{3,2,0,1:T(4,128)(2,1)S(1)}, u32[]{:S(2)}, u32[]{:S(2)}) %all-to-all-start) | async-done | bytes 65568 | tf_op jit(solution)/shard_map/all_to_all | solution.py:85
  29.7 15.8 %all-gather = bf16[1,64,4,1024]{3,2,0,1:T(4,128)(2,1)S(1)} all-gather(bf16[1,64,4,128]{3,2,0,1:T(4,128)(2,1)S(1)} %all-to-all-done), channel_id=2, replica_groups=mesh['cache'=64,'rank'=8] {'rank'}, dimensions={3}, use_global_device_ids=true | all-gather | bytes 589824 | tf_op jit(solution)/shard_map/all_gather | solution.py:86
  47.6 29.7 %while.14 = (s32[]{:T(128)}, f32[64,4,1,128]{3,0,1,2:T(8,128)S(1)}, s32[24]{0:T(128)S(1)}, bf16[24,128,1,128]{3,1,0,2:T(8,128)(2,1)}, bf16[24,128,1,128]{3,1,0,2...) while((s32[]{:T(128)}, f32[64,4,1,128]{3,0,1,2:T(8,128)S(1)}, ...), condition=%wide.region_4.7_spmd.clone, body=%wide.region_3.6_spmd.clone.sunk | while | flops 68226080 | bytes 1646937 | solution.py:61
  47.7 1.7 %gather_fusion = bf16[4,128,128]{2,1,0:T(8,128)(2,1)S(1)} fusion(bf16[24,128,128]{2,1,0:T(8,128)(2,1)} %bitcast.186, s32[1024]{0:T(1024)S(1)} %pad_clamp_fusion.4), kind=kCustom, calls=%fused_computation.3.clone.clone.1 | custom fusion | bytes 262160 | tf_op jit(solution)/shard_map/while/body/eval_jaxpr/jit(_take)/gather | solution.py:44
  49.4 1.7 %gather_fusion.1 = bf16[4,128,128]{2,1,0:T(8,128)(2,1)S(1)} fusion(bf16[24,128,128]{2,1,0:T(8,128)(2,1)} %bitcast.184, s32[1024]{0:T(1024)S(1)} %pad_clamp_fusion.4), kind=kCustom, calls=%fused_computation.1.clone.clone.1 | custom fusion | bytes 262160 | tf_op jit(solution)/shard_map/while/body/eval_jaxpr/jit(_take)/gather | solution.py:47
  51.3 0.7 convert_bitcast_fusion.3
  52.6 1.7 %gather_fusion = bf16[4,128,128]{2,1,0:T(8,128)(2,1)S(1)} fusion(bf16[24,128,128]{2,1,0:T(8,128)(2,1)} %bitcast.186, s32[1024]{0:T(1024)S(1)} %pad_clamp_fusion.4), kind=kCustom, calls=%fused_computation.3.clone.clone.1 | custom fusion | bytes 262160 | tf_op jit(solution)/shard_map/while/body/eval_jaxpr/jit(_take)/gather | solution.py:44
  54.3 1.7 %gather_fusion.1 = bf16[4,128,128]{2,1,0:T(8,128)(2,1)S(1)} fusion(bf16[24,128,128]{2,1,0:T(8,128)(2,1)} %bitcast.184, s32[1024]{0:T(1024)S(1)} %pad_clamp_fusion.4), kind=kCustom, calls=%fused_computation.1.clone.clone.1 | custom fusion | bytes 262160 | tf_op jit(solution)/shard_map/while/body/eval_jaxpr/jit(_take)/gather | solution.py:47
  57.6 1.7 %gather_fusion = bf16[4,128,128]{2,1,0:T(8,128)(2,1)S(1)} fusion(bf16[24,128,128]{2,1,0:T(8,128)(2,1)} %bitcast.186, s32[1024]{0:T(1024)S(1)} %pad_clamp_fusion.4), kind=kCustom, calls=%fused_computation.3.clone.clone.1 | custom fusion | bytes 262160 | tf_op jit(solution)/shard_map/while/body/eval_jaxpr/jit(_take)/gather | solution.py:44
  59.3 1.7 %gather_fusion.1 = bf16[4,128,128]{2,1,0:T(8,128)(2,1)S(1)} fusion(bf16[24,128,128]{2,1,0:T(8,128)(2,1)} %bitcast.184, s32[1024]{0:T(1024)S(1)} %pad_clamp_fusion.4), kind=kCustom, calls=%fused_computation.1.clone.clone.1 | custom fusion | bytes 262160 | tf_op jit(solution)/shard_map/while/body/eval_jaxpr/jit(_take)/gather | solution.py:47
  62.5 1.7 %gather_fusion = bf16[4,128,128]{2,1,0:T(8,128)(2,1)S(1)} fusion(bf16[24,128,128]{2,1,0:T(8,128)(2,1)} %bitcast.186, s32[1024]{0:T(1024)S(1)} %pad_clamp_fusion.4), kind=kCustom, calls=%fused_computation.3.clone.clone.1 | custom fusion | bytes 262160 | tf_op jit(solution)/shard_map/while/body/eval_jaxpr/jit(_take)/gather | solution.py:44
  64.2 1.7 %gather_fusion.1 = bf16[4,128,128]{2,1,0:T(8,128)(2,1)S(1)} fusion(bf16[24,128,128]{2,1,0:T(8,128)(2,1)} %bitcast.184, s32[1024]{0:T(1024)S(1)} %pad_clamp_fusion.4), kind=kCustom, calls=%fused_computation.1.clone.clone.1 | custom fusion | bytes 262160 | tf_op jit(solution)/shard_map/while/body/eval_jaxpr/jit(_take)/gather | solution.py:47
  66.2 0.7 convert_bitcast_fusion.3
  67.5 1.7 %gather_fusion = bf16[4,128,128]{2,1,0:T(8,128)(2,1)S(1)} fusion(bf16[24,128,128]{2,1,0:T(8,128)(2,1)} %bitcast.186, s32[1024]{0:T(1024)S(1)} %pad_clamp_fusion.4), kind=kCustom, calls=%fused_computation.3.clone.clone.1 | custom fusion | bytes 262160 | tf_op jit(solution)/shard_map/while/body/eval_jaxpr/jit(_take)/gather | solution.py:44
  69.2 1.7 %gather_fusion.1 = bf16[4,128,128]{2,1,0:T(8,128)(2,1)S(1)} fusion(bf16[24,128,128]{2,1,0:T(8,128)(2,1)} %bitcast.184, s32[1024]{0:T(1024)S(1)} %pad_clamp_fusion.4), kind=kCustom, calls=%fused_computation.1.clone.clone.1 | custom fusion | bytes 262160 | tf_op jit(solution)/shard_map/while/body/eval_jaxpr/jit(_take)/gather | solution.py:47
  72.4 1.7 %gather_fusion = bf16[4,128,128]{2,1,0:T(8,128)(2,1)S(1)} fusion(bf16[24,128,128]{2,1,0:T(8,128)(2,1)} %bitcast.186, s32[1024]{0:T(1024)S(1)} %pad_clamp_fusion.4), kind=kCustom, calls=%fused_computation.3.clone.clone.1 | custom fusion | bytes 262160 | tf_op jit(solution)/shard_map/while/body/eval_jaxpr/jit(_take)/gather | solution.py:44
  74.1 1.7 %gather_fusion.1 = bf16[4,128,128]{2,1,0:T(8,128)(2,1)S(1)} fusion(bf16[24,128,128]{2,1,0:T(8,128)(2,1)} %bitcast.184, s32[1024]{0:T(1024)S(1)} %pad_clamp_fusion.4), kind=kCustom, calls=%fused_computation.1.clone.clone.1 | custom fusion | bytes 262160 | tf_op jit(solution)/shard_map/while/body/eval_jaxpr/jit(_take)/gather | solution.py:47
  78.6 2.5 %collective-permute-start.1 = (bf16[64,1,4,128]{3,0,2,1:T(8,128)(2,1)S(1)}, bf16[64,1,4,128]{3,0,2,1:T(8,128)(2,1)S(1)}, u32[]{:S(2)}, u32[]{:S(2)}) collective-permute-start(bf16[64,1,4,128]{3,0,2,1:T(8,128)(2,1)S(1)} %bitcast.188), channel_id=1, source_target_pairs={{0,1},{1,2},{2,3},{3,4},{4,5},{5,6},{6,7},{7,0},{8,9},{9,10},{10,1... | collective-permute-start | bytes 196616 | tf_op jit(solution)/shard_map/ppermute | solution.py:21
  81.0 4.0 %collective-permute-start = (bf16[64,1,4,128]{3,0,2,1:T(8,128)(2,1)S(1)}, bf16[64,1,4,128]{3,0,2,1:T(8,128)(2,1)S(1)}, u32[]{:S(2)}, u32[]{:S(2)}) collective-permute-start(bf16[64,1,4,128]{3,0,2,1:T(8,128)(2,1)S(1)} %bitcast.189), channel_id=1, source_target_pairs={{0,7},{1,0},{2,1},{3,2},{4,3},{5,4},{6,5},{7,6},{8,15},{9,8},{10,9... | collective-permute-start | bytes 196616 | tf_op jit(solution)/shard_map/ppermute | solution.py:23
  85.2 1.9 %collective-permute-start.3 = (bf16[64,1,4,128]{3,0,2,1:T(8,128)(2,1)S(1)}, bf16[64,1,4,128]{3,0,2,1:T(8,128)(2,1)S(1)}, u32[]{:S(2)}, u32[]{:S(2)}) collective-permute-start(bf16[64,1,4,128]{3,0,2,1:T(8,128)(2,1)S(1)} %collective-permute-done.1), channel_id=1, source_target_pairs={{0,1},{1,2},{2,3},{3,4},{4,5},{5,6},{6,7},{7,0},{8,9},{9,10},{10,1... | collective-permute-start | bytes 196616 | tf_op jit(solution)/shard_map/ppermute | solution.py:21
  87.2 4.6 %collective-permute-start.2 = (bf16[64,1,4,128]{3,0,2,1:T(8,128)(2,1)S(1)}, bf16[64,1,4,128]{3,0,2,1:T(8,128)(2,1)S(1)}, u32[]{:S(2)}, u32[]{:S(2)}) collective-permute-start(bf16[64,1,4,128]{3,0,2,1:T(8,128)(2,1)S(1)} %collective-permute-done), channel_id=1, source_target_pairs={{0,7},{1,0},{2,1},{3,2},{4,3},{5,4},{6,5},{7,6},{8,15},{9,8},{10,9... | collective-permute-start | bytes 196616 | tf_op jit(solution)/shard_map/ppermute | solution.py:23
  92.1 1.9 %collective-permute-start.5 = (bf16[64,1,4,128]{3,0,2,1:T(8,128)(2,1)S(1)}, bf16[64,1,4,128]{3,0,2,1:T(8,128)(2,1)S(1)}, u32[]{:S(2)}, u32[]{:S(2)}) collective-permute-start(bf16[64,1,4,128]{3,0,2,1:T(8,128)(2,1)S(1)} %collective-permute-done.3), channel_id=1, source_target_pairs={{0,1},{1,2},{2,3},{3,4},{4,5},{5,6},{6,7},{7,0},{8,9},{9,10},{10,1... | collective-permute-start | bytes 196616 | tf_op jit(solution)/shard_map/ppermute | solution.py:21
  94.2 4.6 %collective-permute-start.4 = (bf16[64,1,4,128]{3,0,2,1:T(8,128)(2,1)S(1)}, bf16[64,1,4,128]{3,0,2,1:T(8,128)(2,1)S(1)}, u32[]{:S(2)}, u32[]{:S(2)}) collective-permute-start(bf16[64,1,4,128]{3,0,2,1:T(8,128)(2,1)S(1)} %collective-permute-done.2), channel_id=1, source_target_pairs={{0,7},{1,0},{2,1},{3,2},{4,3},{5,4},{6,5},{7,6},{8,15},{9,8},{10,9... | collective-permute-start | bytes 196616 | tf_op jit(solution)/shard_map/ppermute | solution.py:23
  98.9 1.9 %collective-permute-start.6 = (bf16[64,1,4,128]{3,0,2,1:T(8,128)(2,1)S(1)}, bf16[64,1,4,128]{3,0,2,1:T(8,128)(2,1)S(1)}, u32[]{:S(2)}, u32[]{:S(2)}) collective-permute-start(bf16[64,1,4,128]{3,0,2,1:T(8,128)(2,1)S(1)} %collective-permute-done.5), channel_id=1, source_target_pairs={{0,1},{1,2},{2,3},{3,4},{4,5},{5,6},{6,7},{7,0},{8,9},{9,10},{10,1... | collective-permute-start | bytes 196616 | tf_op jit(solution)/shard_map/ppermute | solution.py:21
  101.2 4.0 %collective-permute-done.6 = bf16[64,1,4,128]{3,0,2,1:T(8,128)(2,1)S(1)} collective-permute-done((bf16[64,1,4,128]{3,0,2,1:T(8,128)(2,1)S(1)}, bf16[64,1,4,128]{3,0,2,1:T(8,128)(2,1)S(1)}, u32[]{:S(2)}, u32[]{:S(2)}) %collective-permute-start.6) | collective-permute-done | bytes 65568 | tf_op jit(solution)/shard_map/ppermute | solution.py:21
  106.0 11.1 %all-to-all-start.1 = ((bf16[64,1,4,128]{3,2,1,0:T(4,128)(2,1)}), bf16[64,1,4,128]{3,2,1,0:T(4,128)(2,1)S(1)}, u32[]{:S(2)}, u32[]{:S(2)}) async-start(bf16[64,1,4,128]{3,2,1,0:T(4,128)(2,1)} %copy.46), calls=%async_computation.1 | async-start | bytes 131072 | tf_op jit(solution)/shard_map/all_to_all | solution.py:65
  117.2 9.9 %all-to-all-done.1 = bf16[64,1,4,128]{3,2,1,0:T(4,128)(2,1)S(1)} async-done(((bf16[64,1,4,128]{3,2,1,0:T(4,128)(2,1)}), bf16[64,1,4,128]{3,2,1,0:T(4,128)(2,1)S(1)}, u32[]{:S(2)}, u32[]{:S(2)}) %all-to-all-start.1) | async-done | bytes 65568 | tf_op jit(solution)/shard_map/all_to_all | solution.py:65
  127.7 0.8 bitcast_select_fusion.2
  (87 shorter events, 14.8 us)
Async XLA Ops:
  0.0 85.1 %copy-start = (bf16[1,1024,128]{2,1,0:T(8,128)(2,1)S(1)}, bf16[1,1024,128]{2,1,0:T(8,128)(2,1)}, u32[]{:S(2)}) copy-start(bf16[1,1024,128]{2,1,0:T(8,128)(2,1)} %param.23) | copy-start | bytes 786436
  0.0 0.7 copy-start.4
  5.0 24.6 %all-to-all-start = ((bf16[1,64,4,128]{3,2,0,1:T(4,128)(2,1)}), bf16[1,64,4,128]{3,2,0,1:T(4,128)(2,1)S(1)}, u32[]{:S(2)}, u32[]{:S(2)}) async-start(bf16[1,64,4,128]{3,2,0,1:T(4,128)(2,1)} %fusion.56), calls=%async_computation | async-start | bytes 131072 | tf_op jit(solution)/shard_map/all_to_all | solution.py:85
  20.7 0.7 copy-start.3
  46.3 1.0 copy-start.1
  77.3 1.0 copy-start.2
  78.6 6.7 %collective-permute-start.1 = (bf16[64,1,4,128]{3,0,2,1:T(8,128)(2,1)S(1)}, bf16[64,1,4,128]{3,0,2,1:T(8,128)(2,1)S(1)}, u32[]{:S(2)}, u32[]{:S(2)}) collective-permute-start(bf16[64,1,4,128]{3,0,2,1:T(8,128)(2,1)S(1)} %bitcast.188), channel_id=1, source_target_pairs={{0,1},{1,2},{2,3},{3,4},{4,5},{5,6},{6,7},{7,0},{8,9},{9,10},{10,1... | collective-permute-start | bytes 196616 | tf_op jit(solution)/shard_map/ppermute | solution.py:21
  81.0 6.1 %collective-permute-start = (bf16[64,1,4,128]{3,0,2,1:T(8,128)(2,1)S(1)}, bf16[64,1,4,128]{3,0,2,1:T(8,128)(2,1)S(1)}, u32[]{:S(2)}, u32[]{:S(2)}) collective-permute-start(bf16[64,1,4,128]{3,0,2,1:T(8,128)(2,1)S(1)} %bitcast.189), channel_id=1, source_target_pairs={{0,7},{1,0},{2,1},{3,2},{4,3},{5,4},{6,5},{7,6},{8,15},{9,8},{10,9... | collective-permute-start | bytes 196616 | tf_op jit(solution)/shard_map/ppermute | solution.py:23
  85.2 6.8 %collective-permute-start.3 = (bf16[64,1,4,128]{3,0,2,1:T(8,128)(2,1)S(1)}, bf16[64,1,4,128]{3,0,2,1:T(8,128)(2,1)S(1)}, u32[]{:S(2)}, u32[]{:S(2)}) collective-permute-start(bf16[64,1,4,128]{3,0,2,1:T(8,128)(2,1)S(1)} %collective-permute-done.1), channel_id=1, source_target_pairs={{0,1},{1,2},{2,3},{3,4},{4,5},{5,6},{6,7},{7,0},{8,9},{9,10},{10,1... | collective-permute-start | bytes 196616 | tf_op jit(solution)/shard_map/ppermute | solution.py:21
  87.2 7.0 %collective-permute-start.2 = (bf16[64,1,4,128]{3,0,2,1:T(8,128)(2,1)S(1)}, bf16[64,1,4,128]{3,0,2,1:T(8,128)(2,1)S(1)}, u32[]{:S(2)}, u32[]{:S(2)}) collective-permute-start(bf16[64,1,4,128]{3,0,2,1:T(8,128)(2,1)S(1)} %collective-permute-done), channel_id=1, source_target_pairs={{0,7},{1,0},{2,1},{3,2},{4,3},{5,4},{6,5},{7,6},{8,15},{9,8},{10,9... | collective-permute-start | bytes 196616 | tf_op jit(solution)/shard_map/ppermute | solution.py:23
  92.1 6.8 %collective-permute-start.5 = (bf16[64,1,4,128]{3,0,2,1:T(8,128)(2,1)S(1)}, bf16[64,1,4,128]{3,0,2,1:T(8,128)(2,1)S(1)}, u32[]{:S(2)}, u32[]{:S(2)}) collective-permute-start(bf16[64,1,4,128]{3,0,2,1:T(8,128)(2,1)S(1)} %collective-permute-done.3), channel_id=1, source_target_pairs={{0,1},{1,2},{2,3},{3,4},{4,5},{5,6},{6,7},{7,0},{8,9},{9,10},{10,1... | collective-permute-start | bytes 196616 | tf_op jit(solution)/shard_map/ppermute | solution.py:21
  94.2 6.8 %collective-permute-start.4 = (bf16[64,1,4,128]{3,0,2,1:T(8,128)(2,1)S(1)}, bf16[64,1,4,128]{3,0,2,1:T(8,128)(2,1)S(1)}, u32[]{:S(2)}, u32[]{:S(2)}) collective-permute-start(bf16[64,1,4,128]{3,0,2,1:T(8,128)(2,1)S(1)} %collective-permute-done.2), channel_id=1, source_target_pairs={{0,7},{1,0},{2,1},{3,2},{4,3},{5,4},{6,5},{7,6},{8,15},{9,8},{10,9... | collective-permute-start | bytes 196616 | tf_op jit(solution)/shard_map/ppermute | solution.py:23
  98.9 6.2 %collective-permute-start.6 = (bf16[64,1,4,128]{3,0,2,1:T(8,128)(2,1)S(1)}, bf16[64,1,4,128]{3,0,2,1:T(8,128)(2,1)S(1)}, u32[]{:S(2)}, u32[]{:S(2)}) collective-permute-start(bf16[64,1,4,128]{3,0,2,1:T(8,128)(2,1)S(1)} %collective-permute-done.5), channel_id=1, source_target_pairs={{0,1},{1,2},{2,3},{3,4},{4,5},{5,6},{6,7},{7,0},{8,9},{9,10},{10,1... | collective-permute-start | bytes 196616 | tf_op jit(solution)/shard_map/ppermute | solution.py:21
  106.0 21.0 %all-to-all-start.1 = ((bf16[64,1,4,128]{3,2,1,0:T(4,128)(2,1)}), bf16[64,1,4,128]{3,2,1,0:T(4,128)(2,1)S(1)}, u32[]{:S(2)}, u32[]{:S(2)}) async-start(bf16[64,1,4,128]{3,2,1,0:T(4,128)(2,1)} %copy.46), calls=%async_computation.1 | async-start | bytes 131072 | tf_op jit(solution)/shard_map/all_to_all | solution.py:65
